TPU v7x, 512 devices: a whole 4x8x8 slice. The times are simulated.
512 devices in a mesh: dp: 32 (over x, y), table: 16 (over z, core).
Axes of the slice: x: 4, y: 8, z: 8, core: 2. Of those that a mesh axis runs over, the one named last changes fastest.
Arguments:
- table: bfloat16 [12288, 512], P('table'), may hold values from -6 to 6
- history_shard: int32 [512, 256, 1], P(('dp', 'table')), may hold values from 0 to 15; in each aligned block of 256 rows (0 to 255, 256 to 511, ..., all dimensions but the last counted through in order) at most 32 rows name the same one
- history_row: int32 [512, 256], P(('dp', 'table')), may hold values from 0 to 767
- lengths: int32 [512], P(('dp', 'table')), may hold values from 1 to 256, 98304 in all
- w_in: bfloat16 [512, 2048], replicated, may hold values from -0.25 to 0.25
- w_out: bfloat16 [512, 512], replicated, may hold values from -0.25 to 0.25
- cotangent: bfloat16 [512, 256, 512], P(('dp', 'table')), may hold values from -6 to 6
Outputs:
- table_grad: float32 [12288, 512], P('table')
- dense_grad: bfloat16 [512, 512], replicated
Inputs may be any that keep to these rules, and one draw needn't show every extreme that they name: `history_shard`: among the 256 history slots of one device's samples, at most 32 name one table shard, and that bound is met by some shard in some device's slots. `lengths`: some sample has the full length 256.
All inputs are finite; a program needn't handle non-finite values. No bound on the sum of `lengths` on one device may be relied on, other than what follows from the above.
Results may differ from a plain program's by a relative error of at most 0.017.
Values may be sent and summed in bfloat16 or wider, within the bound.
A program may use at most 64 MiB of HBM per device.

v0:
```python
import math
import jax
import jax.numpy as jnp
from jax import lax
from jax.sharding import PartitionSpec as P

HEADS = 4


def layer_norm(values):
    average = jnp.mean(values, axis=-1, keepdims=True)
    centred = values - average
    variance = jnp.mean(centred * centred, axis=-1, keepdims=True)
    return centred * lax.rsqrt(variance + 1e-06)


def hstu_layer(embedded, w_in, w_out, lengths):
    samples_here, seq_span, model_width = embedded.shape
    head_dim = model_width // HEADS
    normed = layer_norm(embedded.astype(jnp.float32)).astype(jnp.bfloat16)
    projected = jax.nn.silu(
        jnp.dot(
            normed.reshape(samples_here * seq_span, model_width),
            w_in,
            preferred_element_type=jnp.float32,
        )
    )
    gate_part = projected[:, :model_width]
    shaped = (samples_here, seq_span, HEADS, head_dim)
    values = projected[:, model_width : 2 * model_width].astype(jnp.bfloat16).reshape(shaped)
    queries = projected[:, 2 * model_width : 3 * model_width].astype(jnp.bfloat16).reshape(shaped)
    keys = projected[:, 3 * model_width :].astype(jnp.bfloat16).reshape(shaped)
    scores = jnp.einsum(
        "blhd,bmhd->bhlm", queries.astype(jnp.float32), keys.astype(jnp.float32)
    ) * head_dim ** (-0.5)
    positions = jnp.arange(seq_span)
    live_keys = (positions[None, None, :] <= positions[None, :, None]) & (
        positions[None, None, :] < lengths[:, None, None]
    )
    weights = (
        jnp.where(live_keys[:, None], jax.nn.silu(scores), 0.0)
        / lengths.astype(jnp.float32)[:, None, None, None]
    )
    weights = weights.astype(jnp.bfloat16)
    attended = jnp.einsum(
        "bhlm,bmhd->blhd", weights.astype(jnp.float32), values.astype(jnp.float32)
    ).reshape(samples_here * seq_span, model_width)
    mixed = (layer_norm(attended) * gate_part).astype(jnp.bfloat16)
    output = jnp.dot(mixed, w_out, preferred_element_type=jnp.float32) + embedded.reshape(
        -1, model_width
    ).astype(jnp.float32)
    return (output, mixed)


def pick_rows(index, length):
    return (index[:, None] == jnp.arange(length, dtype=jnp.int32)[None, :]).astype(jnp.bfloat16)


def per_device(table, history_shard, history_row, lengths, w_in, w_out, cotangent):
    shard_rows, model_width = table.shape
    samples_here, seq_span = history_row.shape
    groups = lax.axis_size("table")
    copies = lax.axis_size("dp")
    slot_count = samples_here * seq_span
    capacity = 2 * slot_count // groups
    owners = history_shard[:, :, 0].reshape(-1)
    local_rows = history_row.reshape(-1)
    owner_hits = (owners[:, None] == jnp.arange(groups)[None, :]).astype(jnp.int32)
    slot_rank = jnp.sum((jnp.cumsum(owner_hits, axis=0) - owner_hits) * owner_hits, axis=1)
    position = owners * capacity + slot_rank
    slot_hits = position[:, None] == jnp.arange(groups * capacity, dtype=jnp.int32)[None, :]
    requested = jnp.sum(jnp.where(slot_hits, local_rows[:, None], 0), axis=0).reshape(
        groups, capacity
    )
    incoming = lax.all_to_all(requested, "table", split_axis=0, concat_axis=0, tiled=True).reshape(
        -1
    )
    reply = jnp.dot(
        pick_rows(incoming, shard_rows), table, preferred_element_type=jnp.float32
    ).astype(jnp.bfloat16)
    received = lax.all_to_all(
        reply.reshape(groups, capacity, model_width),
        "table",
        split_axis=0,
        concat_axis=0,
        tiled=True,
    ).reshape(groups * capacity, model_width)
    place = slot_hits.astype(jnp.bfloat16)
    embedded = jnp.dot(place, received, preferred_element_type=jnp.float32).astype(jnp.bfloat16)
    embedded = embedded.reshape(samples_here, seq_span, model_width)
    output, pullback, mixed = jax.vjp(
        lambda rows_in: hstu_layer(rows_in, w_in, w_out, lengths), embedded, has_aux=True
    )
    row_live = jnp.arange(seq_span)[None, :] < lengths[:, None]
    grad_seed = jnp.where(row_live[:, :, None], cotangent, jnp.zeros_like(cotangent))
    flat_seed = grad_seed.reshape(-1, model_width)
    total_slots = slot_count * copies * groups
    grad_scale = 1.0 / math.sqrt(total_slots)
    dense_part = lax.dot_general(
        mixed, flat_seed, (((0,), (0,)), ((), ())), preferred_element_type=jnp.float32
    ).astype(jnp.bfloat16)
    dense_rows = model_width // groups
    dense_terms = lax.all_to_all(
        dense_part.reshape(groups, dense_rows, model_width),
        "table",
        split_axis=0,
        concat_axis=0,
        tiled=True,
    )
    dense_block = jnp.sum(dense_terms.astype(jnp.float32), axis=0).astype(jnp.bfloat16)
    dense_blocks = lax.all_gather(dense_block, "dp", axis=0, tiled=False)
    dense_sum = jnp.sum(dense_blocks.astype(jnp.float32), axis=0) * grad_scale
    dense_grad = lax.all_gather(dense_sum.astype(jnp.bfloat16), "table", axis=0, tiled=True)
    (row_grad,) = pullback(flat_seed.astype(jnp.float32))
    outgoing = lax.dot_general(
        place,
        row_grad.reshape(-1, model_width),
        (((0,), (0,)), ((), ())),
        preferred_element_type=jnp.float32,
    ).astype(jnp.bfloat16)
    arrived = lax.all_to_all(
        outgoing.reshape(groups, capacity, model_width),
        "table",
        split_axis=0,
        concat_axis=0,
        tiled=True,
    ).reshape(groups * capacity, model_width)
    local_grad = lax.dot_general(
        pick_rows(incoming, shard_rows),
        arrived,
        (((0,), (0,)), ((), ())),
        preferred_element_type=jnp.float32,
    ).astype(jnp.bfloat16)
    part_rows = shard_rows // copies
    terms = lax.all_to_all(
        local_grad.reshape(copies, part_rows, model_width),
        "dp",
        split_axis=0,
        concat_axis=0,
        tiled=True,
    )
    summed = jnp.sum(terms.astype(jnp.float32), axis=0).astype(jnp.bfloat16)
    table_grad = lax.all_gather(summed, "dp", axis=0, tiled=True).astype(jnp.float32)
    return (table_grad, dense_grad)


def solution(mesh):
    in_specs = (
        P("table", None),
        P(("dp", "table"), None, None),
        P(("dp", "table"), None),
        P(("dp", "table")),
        P(),
        P(),
        P(("dp", "table"), None, None),
    )
    out_specs = (P("table", None), P())
    return jax.shard_map(
        per_device, mesh=mesh, in_specs=in_specs, out_specs=out_specs, check_vma=False
    )
```

profile of v0, /device:TPU:1, one launch (start us, length us, event | category | flops | bytes accessed | tf_op | source)
XLA Modules:
  0.0 225.5 jit_solution(14855246301839063184)
XLA Ops:
  7.2 0.8 fusion.62
  8.8 0.8 fusion.61
  10.3 0.8 select_reduce_fusion
  11.2 18.6 %all_to_all.29 = s32[16,1,32]{2,1,0:T(1,128)S(1)} all-to-all(s32[16,1,32]{2,1,0:T(1,128)S(1)} %all_to_all.18), channel_id=1, replica_groups=mesh['dp'=32,'table'=16] {'table'}, dimensions={0} | all-to-all | bytes 4096 | tf_op jit(solution)/shard_map/all_to_all | solution.py:75
  31.1 2.5 %fusion.17 = bf16[512,512]{1,0:T(8,128)(2,1)} fusion(bf16[768,512]{1,0:T(8,128)(2,1)} %param.7, s32[512]{0:T(512)S(1)} %eq.68), kind=kOutput, calls=%fused_computation.23 | convolution fusion | flops 403308544 | bytes 1312768 | tf_op jit(solution)/shard_map/dot_general | solution.py:78
  33.6 4.0 %all-to-all-start.1 = ((bf16[16,32,512]{2,1,0:T(8,128)(2,1)}), bf16[16,32,512]{2,1,0:T(8,128)(2,1)S(1)}, u32[]{:S(2)}, u32[]{:S(2)}) async-start(bf16[16,32,512]{2,1,0:T(8,128)(2,1)} %bitcast.6), calls=%async_computation.1 | async-start | bytes 1048576 | tf_op jit(solution)/shard_map/all_to_all | solution.py:81
  38.4 16.6 %all-to-all-done.1 = bf16[16,32,512]{2,1,0:T(8,128)(2,1)S(1)} async-done(((bf16[16,32,512]{2,1,0:T(8,128)(2,1)}), bf16[16,32,512]{2,1,0:T(8,128)(2,1)S(1)}, u32[]{:S(2)}, u32[]{:S(2)}) %all-to-all-start.1) | async-done | bytes 524320 | tf_op jit(solution)/shard_map/all_to_all | solution.py:81
  55.7 2.7 %fusion.70 = (bf16[256,2048]{1,0:T(8,128)(2,1)S(1)}, f32[256,2048]{1,0:T(8,128)}, f32[256,2048]{1,0:T(8,128)}) fusion(bf16[512,2048]{1,0:T(8,128)(2,1)S(1)} %copy-done, f32[256,512]{1,0:T(8,128)S(1)} %get-tuple-element.15, f32[256]{0:T(256)S(1)} %fusion.63, f32[256]{0:T(256)S(1)} %broadcast_multiply_fusion.1), kind=kOutput, calls=%fused_computation.113 | convolution fusion | flops 539885568 | bytes 7866368 | tf_op jit(solution)/shard_map/jvp()/dot_general | solution.py:22
  60.0 1.6 divide_convert_fusion
  62.7 1.2 copy.48
  64.0 1.8 multiply_reduce_fusion.1
  65.9 1.3 convolution_convert_fusion.1
  67.2 1.0 fusion.69
  68.4 1.3 fusion.76
  69.7 2.0 fusion.31
  72.1 0.9 fusion.75
  73.0 0.8 copy.52
  73.9 1.9 copy.50
  75.7 0.9 copy.51
  76.6 4.1 %all-to-all-start.4 = ((bf16[16,32,512]{2,1,0:T(8,128)(2,1)}), bf16[16,32,512]{2,1,0:T(8,128)(2,1)}, u32[]{:S(2)}, u32[]{:S(2)}) async-start(bf16[16,32,512]{2,1,0:T(8,128)(2,1)} %bitcast.30), calls=%async_computation.4 | async-start | bytes 1048576 | tf_op jit(solution)/shard_map/all_to_all | solution.py:103
  80.7 2.9 %multiply_reduce_fusion = (f32[256]{0:T(256)S(1)}, f32[256,512]{1,0:T(8,128)S(1)}) fusion(f32[256,512]{1,0:T(8,128)S(1)} %get-tuple-element.15, f32[256]{0:T(256)S(1)} %broadcast_multiply_fusion.1, bf16[512,2048]{1,0:T(8,128)(2,1)S(1)} %copy-done, f32[256,2048]{1,0:T(8,128)} %get-tuple-element.16, f32[256,512]{1,0:T(8,128)} %get-tuple-element.8, ...), kind=kOutput, calls=%fused_computation.56 | convolution fusion | flops 545390336 | bytes 6555648 | tf_op jit(solution)/shard_map/transpose(jvp())/dot_general | solution.py:22
  84.0 1.3 convolution_convert_fusion.2
  85.3 11.7 %all-to-all-done.4 = bf16[16,32,512]{2,1,0:T(8,128)(2,1)} async-done(((bf16[16,32,512]{2,1,0:T(8,128)(2,1)}), bf16[16,32,512]{2,1,0:T(8,128)(2,1)}, u32[]{:S(2)}, u32[]{:S(2)}) %all-to-all-start.4) | async-done | bytes 524320 | tf_op jit(solution)/shard_map/all_to_all | solution.py:103
  96.9 3.5 %all-to-all-start.2 = ((bf16[16,32,512]{2,1,0:T(8,128)(2,1)}), bf16[16,32,512]{2,1,0:T(8,128)(2,1)S(1)}, u32[]{:S(2)}, u32[]{:S(2)}) async-start(bf16[16,32,512]{2,1,0:T(8,128)(2,1)} %bitcast.27), calls=%async_computation.2 | async-start | bytes 1048576 | tf_op jit(solution)/shard_map/all_to_all | solution.py:121
  100.5 1.7 reduce_sum.150
  102.2 14.9 %all-to-all-done.2 = bf16[16,32,512]{2,1,0:T(8,128)(2,1)S(1)} async-done(((bf16[16,32,512]{2,1,0:T(8,128)(2,1)}), bf16[16,32,512]{2,1,0:T(8,128)(2,1)S(1)}, u32[]{:S(2)}, u32[]{:S(2)}) %all-to-all-start.2) | async-done | bytes 524320 | tf_op jit(solution)/shard_map/all_to_all | solution.py:121
  117.8 31.6 %all_to_all.30 = bf16[32,24,512]{2,1,0:T(8,128)(2,1)S(1)} all-to-all(bf16[32,24,512]{2,1,0:T(8,128)(2,1)S(1)} %bitcast.113), channel_id=1, replica_groups=mesh['dp'=32,'table'=16] {'dp'}, dimensions={0} | all-to-all | bytes 1572864 | tf_op jit(solution)/shard_map/all_to_all | solution.py:135
  149.5 40.4 %all_gather.12 = bf16[768,512]{1,0:T(8,128)(2,1)S(1)} all-gather(bf16[24,512]{1,0:T(8,128)(2,1)S(1)} %reduce_sum.149), channel_id=1, replica_groups=mesh['dp'=32,'table'=16] {'dp'}, dimensions={0}, use_global_device_ids=true | all-gather | bytes 811008 | tf_op jit(solution)/shard_map/all_gather | solution.py:143
  189.9 1.4 convert_element_type.164
  191.3 1.4 convert_reduce_fusion
  192.7 25.2 %all_gather.15 = bf16[512,512]{1,0:T(8,128)(2,1)S(1)} all-gather(bf16[32,512]{1,0:T(8,128)(2,1)S(1)} %multiply_convert_fusion.4), channel_id=1, replica_groups=mesh['dp'=32,'table'=16] {'table'}, dimensions={0}, use_global_device_ids=true | all-gather | bytes 557056 | tf_op jit(solution)/shard_map/all_gather | solution.py:113
  217.9 0.8 copy.70
  (57 shorter events, 8.1 us)
Async XLA Ops:
  7.2 48.5 %copy-start = (bf16[512,2048]{1,0:T(8,128)(2,1)S(1)}, bf16[512,2048]{1,0:T(8,128)(2,1)}, u32[]{:S(2)}) copy-start(bf16[512,2048]{1,0:T(8,128)(2,1)} %param.11) | copy-start | bytes 6291460
  33.6 21.4 %all-to-all-start.1 = ((bf16[16,32,512]{2,1,0:T(8,128)(2,1)}), bf16[16,32,512]{2,1,0:T(8,128)(2,1)S(1)}, u32[]{:S(2)}, u32[]{:S(2)}) async-start(bf16[16,32,512]{2,1,0:T(8,128)(2,1)} %bitcast.6), calls=%async_computation.1 | async-start | bytes 1048576 | tf_op jit(solution)/shard_map/all_to_all | solution.py:81
  59.3 0.7 copy-start.5
  59.4 2.1 copy-start.7
  60.0 1.6 copy-start.9
  61.6 0.8 copy-start.3
  61.6 2.4 %copy-start.2 = (bf16[1,256,512]{2,1,0:T(8,128)(2,1)S(1)}, bf16[1,256,512]{2,1,0:T(8,128)(2,1)}, u32[]{:S(2)}) copy-start(bf16[1,256,512]{2,1,0:T(8,128)(2,1)} %param.13) | copy-start | bytes 786436
  61.9 0.8 copy-start.1
  64.0 1.9 copy-start.4
  69.7 2.1 copy-start.6
  69.7 2.4 %copy-start.8 = (bf16[256,512]{0,1:T(8,128)(2,1)S(1)}, bf16[256,512]{0,1:T(8,128)(2,1)}, u32[]{:S(2)}) copy-start(bf16[256,512]{0,1:T(8,128)(2,1)} %copy-done.7) | copy-start | bytes 786436
  73.9 6.9 %copy-start.10 = (bf16[256,512]{1,0:T(8,128)(2,1)S(1)}, bf16[256,512]{1,0:T(8,128)(2,1)}, u32[]{:S(2)}) copy-start(bf16[256,512]{1,0:T(8,128)(2,1)} %copy.52) | copy-start | bytes 786436
  76.6 20.3 %all-to-all-start.4 = ((bf16[16,32,512]{2,1,0:T(8,128)(2,1)}), bf16[16,32,512]{2,1,0:T(8,128)(2,1)}, u32[]{:S(2)}, u32[]{:S(2)}) async-start(bf16[16,32,512]{2,1,0:T(8,128)(2,1)} %bitcast.30), calls=%async_computation.4 | async-start | bytes 1048576 | tf_op jit(solution)/shard_map/all_to_all | solution.py:103
  96.9 20.2 %all-to-all-start.2 = ((bf16[16,32,512]{2,1,0:T(8,128)(2,1)}), bf16[16,32,512]{2,1,0:T(8,128)(2,1)S(1)}, u32[]{:S(2)}, u32[]{:S(2)}) async-start(bf16[16,32,512]{2,1,0:T(8,128)(2,1)} %bitcast.27), calls=%async_computation.2 | async-start | bytes 1048576 | tf_op jit(solution)/shard_map/all_to_all | solution.py:121
  100.4 90.9 %all-gather.3.cloned.1.call-start = ((), (), s32[]{:S(2)}) async-start(), calls=%async_computation.5 | async-start | bytes 1081344 | tf_op jit(solution)/shard_map/all_gather | solution.py:111
Sparse Core Ops, SparseCore 0:
  104.4 79.3 all-gather.2
where the time goes:
time: 226 us
  blocking collectives  116 us (51%)
  waiting for transfers between devices  43.2 us (19%)
  matrix products  20.1 us (9%)
  between operations  14.9 us (7%)
  starting transfers between devices  11.7 us (5%)
  other arithmetic  10.8 us (5%)
  local copies, waits for them, and re-layouts  8.98 us (4%)
    all_gather x1, blocking collectives, per_device(): lax.all_gather(summed, 'dp', axis=0, tiled=True).astype(jnp.float32)  40.4 us
    all_to_all x1, blocking collectives, per_device(): lax.all_to_all(local_grad.reshape(copies, part_rows, model_width), 'dp',...  31.6 us
    all_gather x1, blocking collectives, per_device(): lax.all_gather(dense_sum.astype(jnp.bfloat16), 'table', axis=0, tiled=True)  25.2 us
    all_to_all x1, blocking collectives, per_device(): lax.all_to_all(requested, 'table', split_axis=0, concat_axis=0, tiled=True)  18.6 us
    all_to_all x1, waiting for transfers between devices, per_device(): lax.all_to_all(reply.reshape(groups, capacity, model_width), 'table', spl...  16.6 us
    all_to_all x1, waiting for transfers between devices, per_device(): lax.all_to_all(outgoing.reshape(groups, capacity, model_width), 'table',...  14.9 us
    all_to_all x1, waiting for transfers between devices, per_device(): lax.all_to_all(dense_part.reshape(groups, dense_rows, model_width), 'tabl...  11.7 us
    dot_general x2, matrix products, hstu_layer(): jnp.dot(normed.reshape(samples_here * seq_span, model_width), w_in, prefe...  5.66 us
  transfers between devices with their start and end apart: 4, of which 3 were waited for; matrix products, arithmetic and copies ran while one was open for 4% of the time, Pallas kernels for 0%

commit v1 on v0

--- a/solution.py
+++ b/solution.py
@@ -5,6 +5,22 @@
 from jax.sharding import PartitionSpec as P
 
 HEADS = 4
+
+
+def gather_around(x, axis, dim):
+    ways, here, step = (lax.axis_size(axis), lax.axis_index(axis), x.shape[dim])
+    shape = [n * ways if d == dim else n for d, n in enumerate(x.shape)]
+    full = lax.dynamic_update_slice_in_dim(jnp.zeros(shape, x.dtype), x, here * step, axis=dim)
+    going_up = going_down = x
+    for far in range(1, ways // 2 + 1):
+        going_up = lax.ppermute(going_up, axis, [(d, (d + 1) % ways) for d in range(ways)])
+        full = lax.dynamic_update_slice_in_dim(full, going_up, (here - far) % ways * step, axis=dim)
+        if 2 * far < ways:
+            going_down = lax.ppermute(going_down, axis, [(d, (d - 1) % ways) for d in range(ways)])
+            full = lax.dynamic_update_slice_in_dim(
+                full, going_down, (here + far) % ways * step, axis=dim
+            )
+    return full
 
 
 def layer_norm(values):
@@ -110,7 +126,7 @@
     dense_block = jnp.sum(dense_terms.astype(jnp.float32), axis=0).astype(jnp.bfloat16)
     dense_blocks = lax.all_gather(dense_block, "dp", axis=0, tiled=False)
     dense_sum = jnp.sum(dense_blocks.astype(jnp.float32), axis=0) * grad_scale
-    dense_grad = lax.all_gather(dense_sum.astype(jnp.bfloat16), "table", axis=0, tiled=True)
+    dense_grad = gather_around(dense_sum.astype(jnp.bfloat16), "table", 0)
     (row_grad,) = pullback(flat_seed.astype(jnp.float32))
     outgoing = lax.dot_general(
         place,

time: 226 us -> 291 us (1.29)
  waiting for transfers between devices: 43.2 us -> 111 us
  blocking collectives: 116 us -> 55.2 us
  starting transfers between devices: 11.7 us -> 58.1 us
  matrix products: 20.1 us -> 24.3 us
    ppermute x0 -> x15, starting transfers between devices: none -> 37.4 us  [the longest x8 24.1 us: gather_around(): lax.ppermute(going_up, axis, [(d, (d + 1) % ways) for d in range(ways)])]
    all_gather x1, waiting for transfers between devices: 0.01 us -> 33.3 us  [per_device(): dense_blocks = lax.all_gather(dense_block, 'dp', axis=0, tiled=False)]
    all_to_all x1 -> x0, blocking collectives: 31.6 us -> none  [per_device(): lax.all_to_all(local_grad.reshape(copies, part_rows, model_width), 'dp',...]
    all_gather x1 -> x0, blocking collectives: 25.2 us -> none  [per_device(): lax.all_gather(dense_sum.astype(jnp.bfloat16), 'table', axis=0, tiled=True)]
    all_to_all x0 -> x1, waiting for transfers between devices: none -> 22.8 us  [per_device(): lax.all_to_all(local_grad.reshape(copies, part_rows, model_width), 'dp',...]
    ppermute x0 -> x15, waiting for transfers between devices: none -> 10.2 us  [the longest x8 8.77 us: gather_around(): lax.ppermute(going_up, axis, [(d, (d + 1) % ways) for d in range(ways)])]
    all_to_all x0 -> x1, starting transfers between devices: none -> 9.67 us  [per_device(): lax.all_to_all(local_grad.reshape(copies, part_rows, model_width), 'dp',...]
    all_gather x1, blocking collectives: 40.4 us -> 36.6 us  [per_device(): lax.all_gather(summed, 'dp', axis=0, tiled=True).astype(jnp.float32)]
  transfers between devices with their start and end apart: 4 -> 20, of which waited for: 3 -> 18; matrix products, arithmetic and copies ran while one was open for 4% -> 3% of each run, Pallas kernels for 0% -> 0%
where the time goes in v1:
time: 291 us; the launch traced here: 288 us
  waiting for transfers between devices  111 us (38%)
  starting transfers between devices  58.1 us (20%)
  blocking collectives  55.2 us (19%)
  matrix products  24.3 us (8%)
  between operations  15.2 us (5%)
  other arithmetic  12.6 us (4%)
  local copies, waits for them, and re-layouts  11.8 us (4%)
    all_gather x1, blocking collectives, per_device(): lax.all_gather(summed, 'dp', axis=0, tiled=True).astype(jnp.float32)  36.6 us
    all_gather x1, waiting for transfers between devices, per_device(): dense_blocks = lax.all_gather(dense_block, 'dp', axis=0, tiled=False)  33.3 us
    ppermute x8, starting transfers between devices, gather_around(): lax.ppermute(going_up, axis, [(d, (d + 1) % ways) for d in range(ways)])  24.1 us
    all_to_all x1, waiting for transfers between devices, per_device(): lax.all_to_all(local_grad.reshape(copies, part_rows, model_width), 'dp',...  22.8 us
    all_to_all x1, blocking collectives, per_device(): lax.all_to_all(requested, 'table', split_axis=0, concat_axis=0, tiled=True)  18.6 us
    all_to_all x1, waiting for transfers between devices, per_device(): lax.all_to_all(reply.reshape(groups, capacity, model_width), 'table', spl...  16.6 us
    all_to_all x1, waiting for transfers between devices, per_device(): lax.all_to_all(outgoing.reshape(groups, capacity, model_width), 'table',...  16 us
    ppermute x7, starting transfers between devices, gather_around(): lax.ppermute(going_down, axis, [(d, (d - 1) % ways) for d in range(ways)])  13.3 us
  transfers between devices with their start and end apart: 20, of which 18 were waited for; matrix products, arithmetic and copies ran while one was open for 3% of the time, Pallas kernels for 0%

profile of v1, /device:TPU:1, one launch (start us, length us, event | category | flops | bytes accessed | tf_op | source)
XLA Modules:
  0.0 288.3 jit_solution(2841930398637283813)
XLA Ops:
  11.2 18.6 %all_to_all.29 = s32[16,1,32]{2,1,0:T(1,128)S(1)} all-to-all(s32[16,1,32]{2,1,0:T(1,128)S(1)} %all_to_all.18), channel_id=1, replica_groups=mesh['dp'=32,'table'=16] {'table'}, dimensions={0} | all-to-all | bytes 4096 | tf_op jit(solution)/shard_map/all_to_all | solution.py:91
  31.1 2.5 fusion.17
  33.6 4.0 %all-to-all-start.1 = ((bf16[16,32,512]{2,1,0:T(8,128)(2,1)}), bf16[16,32,512]{2,1,0:T(8,128)(2,1)S(1)}, u32[]{:S(2)}, u32[]{:S(2)}) async-start(bf16[16,32,512]{2,1,0:T(8,128)(2,1)} %bitcast.6), calls=%async_computation.1 | async-start | bytes 1048576 | tf_op jit(solution)/shard_map/all_to_all | solution.py:97
  38.4 16.6 %all-to-all-done.1 = bf16[16,32,512]{2,1,0:T(8,128)(2,1)S(1)} async-done(((bf16[16,32,512]{2,1,0:T(8,128)(2,1)}), bf16[16,32,512]{2,1,0:T(8,128)(2,1)S(1)}, u32[]{:S(2)}, u32[]{:S(2)}) %all-to-all-start.1) | async-done | bytes 524320 | tf_op jit(solution)/shard_map/all_to_all | solution.py:97
  55.7 2.7 fusion.70
  65.1 1.6 multiply_reduce_fusion.1
  66.7 2.1 fusion.69
  69.6 1.8 copy.49
  71.4 2.1 fusion.76
  73.5 2.1 fusion.31
  77.6 2.3 convolution_convert_fusion.1
  79.9 1.8 copy.52
  81.7 1.8 copy.51
  83.5 1.8 copy.50
  85.3 3.5 %all-to-all-start.4 = ((bf16[16,32,512]{2,1,0:T(8,128)(2,1)}), bf16[16,32,512]{2,1,0:T(8,128)(2,1)S(1)}, u32[]{:S(2)}, u32[]{:S(2)}) async-start(bf16[16,32,512]{2,1,0:T(8,128)(2,1)} %bitcast.102), calls=%async_computation.4 | async-start | bytes 1048576 | tf_op jit(solution)/shard_map/all_to_all | solution.py:119
  88.8 3.0 %multiply_reduce_fusion = (f32[256]{0:T(256)S(1)}, f32[256,512]{1,0:T(8,128)S(1)}) fusion(f32[256,512]{1,0:T(8,128)S(1)} %get-tuple-element.17, f32[256]{0:T(256)S(1)} %broadcast_multiply_fusion.1, bf16[512,2048]{1,0:T(8,128)(2,1)S(1)} %copy-done, f32[256,2048]{1,0:T(8,128)} %get-tuple-element.18, f32[256,512]{1,0:T(8,128)} %get-tuple-element.10, ...), kind=kOutput, calls=%fused_computation.56 | convolution fusion | flops 545390336 | bytes 6555648 | tf_op jit(solution)/shard_map/transpose(jvp())/dot_general | solution.py:38
  93.4 12.1 %all-to-all-done.4 = bf16[16,32,512]{2,1,0:T(8,128)(2,1)S(1)} async-done(((bf16[16,32,512]{2,1,0:T(8,128)(2,1)}), bf16[16,32,512]{2,1,0:T(8,128)(2,1)S(1)}, u32[]{:S(2)}, u32[]{:S(2)}) %all-to-all-start.4) | async-done | bytes 524320 | tf_op jit(solution)/shard_map/all_to_all | solution.py:119
  105.5 3.5 %all-to-all-start.2 = ((bf16[16,32,512]{2,1,0:T(8,128)(2,1)}), bf16[16,32,512]{2,1,0:T(8,128)(2,1)S(1)}, u32[]{:S(2)}, u32[]{:S(2)}) async-start(bf16[16,32,512]{2,1,0:T(8,128)(2,1)} %bitcast.27), calls=%async_computation.2 | async-start | bytes 1048576 | tf_op jit(solution)/shard_map/all_to_all | solution.py:137
  109.7 16.0 %all-to-all-done.2 = bf16[16,32,512]{2,1,0:T(8,128)(2,1)S(1)} async-done(((bf16[16,32,512]{2,1,0:T(8,128)(2,1)}), bf16[16,32,512]{2,1,0:T(8,128)(2,1)S(1)}, u32[]{:S(2)}, u32[]{:S(2)}) %all-to-all-start.2) | async-done | bytes 524320 | tf_op jit(solution)/shard_map/all_to_all | solution.py:137
  125.7 1.6 fusion.16
  127.3 9.7 %all-to-all-start.3 = ((bf16[32,24,512]{2,1,0:T(8,128)(2,1)}), bf16[32,24,512]{2,1,0:T(8,128)(2,1)S(1)}, u32[]{:S(2)}, u32[]{:S(2)}) async-start(bf16[32,24,512]{2,1,0:T(8,128)(2,1)} %bitcast.114), calls=%async_computation.3 | async-start | bytes 1572864 | tf_op jit(solution)/shard_map/all_to_all | solution.py:151
  137.3 22.8 %all-to-all-done.3 = bf16[32,24,512]{2,1,0:T(8,128)(2,1)S(1)} async-done(((bf16[32,24,512]{2,1,0:T(8,128)(2,1)}), bf16[32,24,512]{2,1,0:T(8,128)(2,1)S(1)}, u32[]{:S(2)}, u32[]{:S(2)}) %all-to-all-start.3) | async-done | bytes 786464 | tf_op jit(solution)/shard_map/all_to_all | solution.py:151
  160.2 33.3 %all-gather.3.cloned.1.call-done = bf16[1024,512]{1,0:T(8,128)(2,1)} async-done(((bf16[32,512]{1,0:T(8,128)(2,1)}), bf16[1024,512]{1,0:T(8,128)(2,1)}) %all-gather.3.cloned.1.call-update) | async-done | bytes 1048592 | tf_op jit(solution)/shard_map/all_gather | solution.py:127
  195.0 6.3 %collective-permute-start = (bf16[32,512]{1,0:T(8,128)(2,1)S(1)}, bf16[32,512]{1,0:T(8,128)(2,1)S(1)}, u32[]{:S(2)}, u32[]{:S(2)}) collective-permute-start(bf16[32,512]{1,0:T(8,128)(2,1)S(1)} %get-tuple-element.3), channel_id=1, source_target_pairs={{0,1},{1,2},{2,3},{3,4},{4,5},{5,6},{6,7},{7,8},{8,9},{9,10},{10,1... | collective-permute-start | bytes 98312 | tf_op jit(solution)/shard_map/ppermute | solution.py:16
  201.3 36.6 %all_gather.9 = bf16[768,512]{1,0:T(8,128)(2,1)S(1)} all-gather(bf16[24,512]{1,0:T(8,128)(2,1)S(1)} %reduce_sum.149), channel_id=1, replica_groups=mesh['dp'=32,'table'=16] {'dp'}, dimensions={0}, use_global_device_ids=true | all-gather | bytes 811008 | tf_op jit(solution)/shard_map/all_gather | solution.py:159
  239.2 13.6 %collective-permute-start.2 = (bf16[32,512]{1,0:T(8,128)(2,1)S(1)}, bf16[32,512]{1,0:T(8,128)(2,1)S(1)}, u32[]{:S(2)}, u32[]{:S(2)}) collective-permute-start(bf16[32,512]{1,0:T(8,128)(2,1)S(1)} %collective-permute-done), channel_id=1, source_target_pairs={{0,1},{1,2},{2,3},{3,4},{4,5},{5,6},{6,7},{7,8},{8,9},{9,10},{10,1... | collective-permute-start | bytes 98312 | tf_op jit(solution)/shard_map/ppermute | solution.py:16
  253.8 2.3 collective-permute-start.4
  259.8 2.0 collective-permute-start.7
  263.1 3.2 %collective-permute-start.9 = (bf16[32,512]{1,0:T(8,128)(2,1)S(1)}, bf16[32,512]{1,0:T(8,128)(2,1)S(1)}, u32[]{:S(2)}, u32[]{:S(2)}) collective-permute-start(bf16[32,512]{1,0:T(8,128)(2,1)S(1)} %collective-permute-done.7), channel_id=1, source_target_pairs={{0,15},{1,0},{2,1},{3,2},{4,3},{5,4},{6,5},{7,6},{8,7},{9,8},{10,9... | collective-permute-start | bytes 98312 | tf_op jit(solution)/shard_map/ppermute | solution.py:19
  267.2 3.7 %collective-permute-start.11 = (bf16[32,512]{1,0:T(8,128)(2,1)S(1)}, bf16[32,512]{1,0:T(8,128)(2,1)S(1)}, u32[]{:S(2)}, u32[]{:S(2)}) collective-permute-start(bf16[32,512]{1,0:T(8,128)(2,1)S(1)} %collective-permute-done.9), channel_id=1, source_target_pairs={{0,15},{1,0},{2,1},{3,2},{4,3},{5,4},{6,5},{7,6},{8,7},{9,8},{10,9... | collective-permute-start | bytes 98312 | tf_op jit(solution)/shard_map/ppermute | solution.py:19
  271.7 3.7 %collective-permute-start.13 = (bf16[32,512]{1,0:T(8,128)(2,1)S(1)}, bf16[32,512]{1,0:T(8,128)(2,1)S(1)}, u32[]{:S(2)}, u32[]{:S(2)}) collective-permute-start(bf16[32,512]{1,0:T(8,128)(2,1)S(1)} %collective-permute-done.11), channel_id=1, source_target_pairs={{0,15},{1,0},{2,1},{3,2},{4,3},{5,4},{6,5},{7,6},{8,7},{9,8},{10,9... | collective-permute-start | bytes 98312 | tf_op jit(solution)/shard_map/ppermute | solution.py:19
  276.3 4.4 %collective-permute-done.14 = bf16[32,512]{1,0:T(8,128)(2,1)S(1)} collective-permute-done((bf16[32,512]{1,0:T(8,128)(2,1)S(1)}, bf16[32,512]{1,0:T(8,128)(2,1)S(1)}, u32[]{:S(2)}, u32[]{:S(2)}) %collective-permute-start.14) | collective-permute-done | bytes 32800 | tf_op jit(solution)/shard_map/ppermute | solution.py:16
  (98 shorter events, 30.0 us)
Async XLA Ops:
  7.2 48.5 %copy-start = (bf16[512,2048]{1,0:T(8,128)(2,1)S(1)}, bf16[512,2048]{1,0:T(8,128)(2,1)}, u32[]{:S(2)}) copy-start(bf16[512,2048]{1,0:T(8,128)(2,1)} %param.11) | copy-start | bytes 6291460
  33.6 21.4 %all-to-all-start.1 = ((bf16[16,32,512]{2,1,0:T(8,128)(2,1)}), bf16[16,32,512]{2,1,0:T(8,128)(2,1)S(1)}, u32[]{:S(2)}, u32[]{:S(2)}) async-start(bf16[16,32,512]{2,1,0:T(8,128)(2,1)} %bitcast.6), calls=%async_computation.1 | async-start | bytes 1048576 | tf_op jit(solution)/shard_map/all_to_all | solution.py:97
  59.3 0.7 copy-start.3
  59.4 2.1 copy-start.5
  60.0 1.6 copy-start.7
  61.6 1.1 copy-start.2
  61.6 3.5 %copy-start.1 = (bf16[1,256,512]{2,1,0:T(8,128)(2,1)S(1)}, bf16[1,256,512]{2,1,0:T(8,128)(2,1)}, u32[]{:S(2)}) copy-start(bf16[1,256,512]{2,1,0:T(8,128)(2,1)} %param.13) | copy-start | bytes 786436
  73.5 2.1 copy-start.6
  73.5 3.1 %copy-start.4 = (bf16[256,512]{0,1:T(8,128)(2,1)S(1)}, bf16[256,512]{0,1:T(8,128)(2,1)}, u32[]{:S(2)}) copy-start(bf16[256,512]{0,1:T(8,128)(2,1)} %copy-done.3) | copy-start | bytes 786436
  85.3 20.2 %all-to-all-start.4 = ((bf16[16,32,512]{2,1,0:T(8,128)(2,1)}), bf16[16,32,512]{2,1,0:T(8,128)(2,1)S(1)}, u32[]{:S(2)}, u32[]{:S(2)}) async-start(bf16[16,32,512]{2,1,0:T(8,128)(2,1)} %bitcast.102), calls=%async_computation.4 | async-start | bytes 1048576 | tf_op jit(solution)/shard_map/all_to_all | solution.py:119
  105.5 20.2 %all-to-all-start.2 = ((bf16[16,32,512]{2,1,0:T(8,128)(2,1)}), bf16[16,32,512]{2,1,0:T(8,128)(2,1)S(1)}, u32[]{:S(2)}, u32[]{:S(2)}) async-start(bf16[16,32,512]{2,1,0:T(8,128)(2,1)} %bitcast.27), calls=%async_computation.2 | async-start | bytes 1048576 | tf_op jit(solution)/shard_map/all_to_all | solution.py:137
  109.0 84.6 %all-gather.3.cloned.1.call-start = ((), (), s32[]{:S(2)}) async-start(), calls=%async_computation.5 | async-start | bytes 1081344 | tf_op jit(solution)/shard_map/all_gather | solution.py:127
  127.3 32.8 %all-to-all-start.3 = ((bf16[32,24,512]{2,1,0:T(8,128)(2,1)}), bf16[32,24,512]{2,1,0:T(8,128)(2,1)S(1)}, u32[]{:S(2)}, u32[]{:S(2)}) async-start(bf16[32,24,512]{2,1,0:T(8,128)(2,1)} %bitcast.114), calls=%async_computation.3 | async-start | bytes 1572864 | tf_op jit(solution)/shard_map/all_to_all | solution.py:151
  195.0 44.2 %collective-permute-start = (bf16[32,512]{1,0:T(8,128)(2,1)S(1)}, bf16[32,512]{1,0:T(8,128)(2,1)S(1)}, u32[]{:S(2)}, u32[]{:S(2)}) collective-permute-start(bf16[32,512]{1,0:T(8,128)(2,1)S(1)} %get-tuple-element.3), channel_id=1, source_target_pairs={{0,1},{1,2},{2,3},{3,4},{4,5},{5,6},{6,7},{7,8},{8,9},{9,10},{10,1... | collective-permute-start | bytes 98312 | tf_op jit(solution)/shard_map/ppermute | solution.py:16
  201.3 51.5 %collective-permute-start.1 = (bf16[32,512]{1,0:T(8,128)(2,1)S(1)}, bf16[32,512]{1,0:T(8,128)(2,1)S(1)}, u32[]{:S(2)}, u32[]{:S(2)}) collective-permute-start(bf16[32,512]{1,0:T(8,128)(2,1)S(1)} %get-tuple-element.3), channel_id=1, source_target_pairs={{0,15},{1,0},{2,1},{3,2},{4,3},{5,4},{6,5},{7,6},{8,7},{9,8},{10,9... | collective-permute-start | bytes 98312 | tf_op jit(solution)/shard_map/ppermute | solution.py:19
  239.2 14.6 %collective-permute-start.2 = (bf16[32,512]{1,0:T(8,128)(2,1)S(1)}, bf16[32,512]{1,0:T(8,128)(2,1)S(1)}, u32[]{:S(2)}, u32[]{:S(2)}) collective-permute-start(bf16[32,512]{1,0:T(8,128)(2,1)S(1)} %collective-permute-done), channel_id=1, source_target_pairs={{0,1},{1,2},{2,3},{3,4},{4,5},{5,6},{6,7},{7,8},{8,9},{9,10},{10,1... | collective-permute-start | bytes 98312 | tf_op jit(solution)/shard_map/ppermute | solution.py:16
  252.8 3.6 %collective-permute-start.3 = (bf16[32,512]{1,0:T(8,128)(2,1)S(1)}, bf16[32,512]{1,0:T(8,128)(2,1)S(1)}, u32[]{:S(2)}, u32[]{:S(2)}) collective-permute-start(bf16[32,512]{1,0:T(8,128)(2,1)S(1)} %collective-permute-done.1), channel_id=1, source_target_pairs={{0,15},{1,0},{2,1},{3,2},{4,3},{5,4},{6,5},{7,6},{8,7},{9,8},{10,9... | collective-permute-start | bytes 98312 | tf_op jit(solution)/shard_map/ppermute | solution.py:19
  253.8 4.1 %collective-permute-start.4 = (bf16[32,512]{1,0:T(8,128)(2,1)S(1)}, bf16[32,512]{1,0:T(8,128)(2,1)S(1)}, u32[]{:S(2)}, u32[]{:S(2)}) collective-permute-start(bf16[32,512]{1,0:T(8,128)(2,1)S(1)} %collective-permute-done.2), channel_id=1, source_target_pairs={{0,1},{1,2},{2,3},{3,4},{4,5},{5,6},{6,7},{7,8},{8,9},{9,10},{10,1... | collective-permute-start | bytes 98312 | tf_op jit(solution)/shard_map/ppermute | solution.py:16
  256.4 3.3 %collective-permute-start.5 = (bf16[32,512]{1,0:T(8,128)(2,1)S(1)}, bf16[32,512]{1,0:T(8,128)(2,1)S(1)}, u32[]{:S(2)}, u32[]{:S(2)}) collective-permute-start(bf16[32,512]{1,0:T(8,128)(2,1)S(1)} %collective-permute-done.3), channel_id=1, source_target_pairs={{0,15},{1,0},{2,1},{3,2},{4,3},{5,4},{6,5},{7,6},{8,7},{9,8},{10,9... | collective-permute-start | bytes 98312 | tf_op jit(solution)/shard_map/ppermute | solution.py:19
  257.9 4.6 %collective-permute-start.6 = (bf16[32,512]{1,0:T(8,128)(2,1)S(1)}, bf16[32,512]{1,0:T(8,128)(2,1)S(1)}, u32[]{:S(2)}, u32[]{:S(2)}) collective-permute-start(bf16[32,512]{1,0:T(8,128)(2,1)S(1)} %collective-permute-done.4), channel_id=1, source_target_pairs={{0,1},{1,2},{2,3},{3,4},{4,5},{5,6},{6,7},{7,8},{8,9},{9,10},{10,1... | collective-permute-start | bytes 98312 | tf_op jit(solution)/shard_map/ppermute | solution.py:16
  259.8 3.3 %collective-permute-start.7 = (bf16[32,512]{1,0:T(8,128)(2,1)S(1)}, bf16[32,512]{1,0:T(8,128)(2,1)S(1)}, u32[]{:S(2)}, u32[]{:S(2)}) collective-permute-start(bf16[32,512]{1,0:T(8,128)(2,1)S(1)} %collective-permute-done.5), channel_id=1, source_target_pairs={{0,15},{1,0},{2,1},{3,2},{4,3},{5,4},{6,5},{7,6},{8,7},{9,8},{10,9... | collective-permute-start | bytes 98312 | tf_op jit(solution)/shard_map/ppermute | solution.py:19
  262.5 4.6 %collective-permute-start.8 = (bf16[32,512]{1,0:T(8,128)(2,1)S(1)}, bf16[32,512]{1,0:T(8,128)(2,1)S(1)}, u32[]{:S(2)}, u32[]{:S(2)}) collective-permute-start(bf16[32,512]{1,0:T(8,128)(2,1)S(1)} %collective-permute-done.6), channel_id=1, source_target_pairs={{0,1},{1,2},{2,3},{3,4},{4,5},{5,6},{6,7},{7,8},{8,9},{9,10},{10,1... | collective-permute-start | bytes 98312 | tf_op jit(solution)/shard_map/ppermute | solution.py:16
  263.1 4.1 %collective-permute-start.9 = (bf16[32,512]{1,0:T(8,128)(2,1)S(1)}, bf16[32,512]{1,0:T(8,128)(2,1)S(1)}, u32[]{:S(2)}, u32[]{:S(2)}) collective-permute-start(bf16[32,512]{1,0:T(8,128)(2,1)S(1)} %collective-permute-done.7), channel_id=1, source_target_pairs={{0,15},{1,0},{2,1},{3,2},{4,3},{5,4},{6,5},{7,6},{8,7},{9,8},{10,9... | collective-permute-start | bytes 98312 | tf_op jit(solution)/shard_map/ppermute | solution.py:19
  267.0 4.6 %collective-permute-start.10 = (bf16[32,512]{1,0:T(8,128)(2,1)S(1)}, bf16[32,512]{1,0:T(8,128)(2,1)S(1)}, u32[]{:S(2)}, u32[]{:S(2)}) collective-permute-start(bf16[32,512]{1,0:T(8,128)(2,1)S(1)} %collective-permute-done.8), channel_id=1, source_target_pairs={{0,1},{1,2},{2,3},{3,4},{4,5},{5,6},{6,7},{7,8},{8,9},{9,10},{10,1... | collective-permute-start | bytes 98312 | tf_op jit(solution)/shard_map/ppermute | solution.py:16
  267.2 4.6 %collective-permute-start.11 = (bf16[32,512]{1,0:T(8,128)(2,1)S(1)}, bf16[32,512]{1,0:T(8,128)(2,1)S(1)}, u32[]{:S(2)}, u32[]{:S(2)}) collective-permute-start(bf16[32,512]{1,0:T(8,128)(2,1)S(1)} %collective-permute-done.9), channel_id=1, source_target_pairs={{0,15},{1,0},{2,1},{3,2},{4,3},{5,4},{6,5},{7,6},{8,7},{9,8},{10,9... | collective-permute-start | bytes 98312 | tf_op jit(solution)/shard_map/ppermute | solution.py:19
  271.6 4.6 %collective-permute-start.12 = (bf16[32,512]{1,0:T(8,128)(2,1)S(1)}, bf16[32,512]{1,0:T(8,128)(2,1)S(1)}, u32[]{:S(2)}, u32[]{:S(2)}) collective-permute-start(bf16[32,512]{1,0:T(8,128)(2,1)S(1)} %collective-permute-done.10), channel_id=1, source_target_pairs={{0,1},{1,2},{2,3},{3,4},{4,5},{5,6},{6,7},{7,8},{8,9},{9,10},{10,1... | collective-permute-start | bytes 98312 | tf_op jit(solution)/shard_map/ppermute | solution.py:16
  271.7 4.6 %collective-permute-start.13 = (bf16[32,512]{1,0:T(8,128)(2,1)S(1)}, bf16[32,512]{1,0:T(8,128)(2,1)S(1)}, u32[]{:S(2)}, u32[]{:S(2)}) collective-permute-start(bf16[32,512]{1,0:T(8,128)(2,1)S(1)} %collective-permute-done.11), channel_id=1, source_target_pairs={{0,15},{1,0},{2,1},{3,2},{4,3},{5,4},{6,5},{7,6},{8,7},{9,8},{10,9... | collective-permute-start | bytes 98312 | tf_op jit(solution)/shard_map/ppermute | solution.py:19
  276.1 4.6 %collective-permute-start.14 = (bf16[32,512]{1,0:T(8,128)(2,1)S(1)}, bf16[32,512]{1,0:T(8,128)(2,1)S(1)}, u32[]{:S(2)}, u32[]{:S(2)}) collective-permute-start(bf16[32,512]{1,0:T(8,128)(2,1)S(1)} %collective-permute-done.12), channel_id=1, source_target_pairs={{0,1},{1,2},{2,3},{3,4},{4,5},{5,6},{6,7},{7,8},{8,9},{9,10},{10,1... | collective-permute-start | bytes 98312 | tf_op jit(solution)/shard_map/ppermute | solution.py:16
  280.7 0.8 copy-start.8
Sparse Core Ops, SparseCore 0:
  113.0 80.5 all-gather.2
